TPU v7x, 32 devices: a whole 2x2x4 slice. The times are simulated.
32 devices in a mesh: blk: 2 (over y), fsdp: 16 (over z, x, core).
Axes of the slice: x: 2, y: 2, z: 4, core: 2. Of those that a mesh axis runs over, the one named last changes fastest.
Arguments:
- tokens: bfloat16 [2, 2048, 2304], P('blk', 'fsdp'), may hold values from -6 to 6
- cotangent: bfloat16 [2, 2048, 512], P('blk', 'fsdp'), may hold values from -6 to 6
- weights: float32 [2, 2304, 512], P('blk', 'fsdp'), may hold values from -6 to 6
- moment_one: float32 [2, 2304, 512], P('blk', 'fsdp'), may hold values from -6 to 6
- moment_two: float32 [2, 2304, 512], P('blk', 'fsdp'), may hold values from 1 to 16
- gossip: int32 [2, 3], P('blk'), may hold values from 1 to 8
Outputs:
- key_out: bfloat16 [2, 2048, 512], P('blk', 'fsdp')
- input_grad: bfloat16 [2, 2048, 2304], P('blk', 'fsdp')
- weights_out: float32 [2, 2304, 512], P('blk', 'fsdp')
- moment_one_out: float32 [2, 2304, 512], P('blk', 'fsdp')
- moment_two_out: float32 [2, 2304, 512], P('blk', 'fsdp')
Inputs may be any that keep to these rules, and one draw needn't show every extreme that they name: `gossip`: row r holds the weights given to replica r - 1, to replica r itself and to replica r + 1 on the closed cycle of 2 replicas.
All inputs are finite; a program needn't handle non-finite values.
Results may differ from a plain program's by a relative error of at most 0.005.
Values may be sent and summed in bfloat16 or wider, within the bound.
A program may use at most 64 MiB of HBM per device.

v0:
```python
import math

import jax
import jax.numpy as jnp
from jax import lax
from jax.sharding import PartitionSpec as P

beta_one = 0.9
beta_two = 0.95
learn_rate = 0.05
weight_decay = 0.1
epsilon = 1e-08
correct_one = 1.0 - beta_one**5
correct_two = 1.0 - beta_two**5


def from_behind(shard, axis, by):
    length = lax.axis_size(axis)
    return lax.ppermute(shard, axis, [(i, (i + by) % length) for i in range(length)])


def local(tokens, cotangent, weights, moment_one, moment_two, gossip):
    activations = tokens[0]
    upstream = cotangent[0]
    factor = 1.0 / math.sqrt(activations.shape[1])
    compute_weights = weights[0].astype(jnp.bfloat16)
    key_sum = jnp.dot(
        activations,
        lax.all_gather(compute_weights, "fsdp", axis=0, tiled=True),
        preferred_element_type=jnp.float32,
    )
    key_out = (key_sum * factor).astype(jnp.bfloat16)
    product = lax.dot_general(
        upstream,
        lax.all_gather(compute_weights, "fsdp", axis=0, tiled=True),
        (((1,), (1,)), ((), ())),
        preferred_element_type=jnp.float32,
    )
    input_grad = (product * factor).astype(jnp.bfloat16)
    owned_inputs = lax.all_to_all(activations, "fsdp", split_axis=1, concat_axis=0, tiled=True)
    gradient = (
        lax.dot_general(
            owned_inputs,
            lax.all_gather(upstream, "fsdp", axis=0, tiled=True),
            (((0,), (0,)), ((), ())),
            preferred_element_type=jnp.float32,
        )
        * factor
    )
    master = weights[0]
    moment_one_out = beta_one * moment_one[0] + (1.0 - beta_one) * gradient
    moment_two_out = beta_two * moment_two[0] + (1.0 - beta_two) * gradient * gradient
    update = moment_one_out / correct_one / (jnp.sqrt(moment_two_out / correct_two) + epsilon)
    stepped = master - learn_rate * (update + weight_decay * master)
    left_side = from_behind(stepped.astype(jnp.bfloat16), "blk", 1).astype(stepped.dtype)
    right_side = from_behind(stepped.astype(jnp.bfloat16), "blk", -1).astype(stepped.dtype)
    mix_weights = gossip[0].astype(jnp.float32)
    averaged = (
        mix_weights[0] * left_side + mix_weights[1] * stepped + mix_weights[2] * right_side
    ) / (mix_weights[0] + mix_weights[1] + mix_weights[2])
    averaged, moment_one_out, moment_two_out = (averaged, moment_one_out, moment_two_out)
    return (
        key_out[None],
        input_grad[None],
        averaged[None],
        moment_one_out[None],
        moment_two_out[None],
    )


def solution(mesh):
    in_specs = (
        P("blk", "fsdp", None),
        P("blk", "fsdp", None),
        P("blk", "fsdp", None),
        P("blk", "fsdp", None),
        P("blk", "fsdp", None),
        P("blk", None),
    )
    out_specs = (
        P("blk", "fsdp", None),
        P("blk", "fsdp", None),
        P("blk", "fsdp", None),
        P("blk", "fsdp", None),
        P("blk", "fsdp", None),
    )
    return jax.shard_map(local, mesh=mesh, in_specs=in_specs, out_specs=out_specs, check_vma=False)
```

profile of v0, /device:TPU:0, one launch (start us, length us, event | category | flops | bytes accessed | tf_op | source)
XLA Modules:
  0.0 113.2 jit_solution(10622832884411012266)
XLA Ops:
  7.2 0.0 copy-start.3
  7.2 0.0 copy-start.4
  7.2 0.0 copy-start.5
  7.2 0.0 all-gather.6.cloned.1.call-start
  7.2 0.7 all-gather.6.cloned.1.call-update
  7.9 0.0 all-gather.4.cloned.1.call-start
  8.0 1.6 %bitcast_convert_fusion = bf16[144,512]{1,0:T(8,128)(2,1)} fusion(f32[1,144,512]{2,1,0:T(8,128)} %param.8), kind=kLoop, calls=%fused_computation.21 | loop fusion | flops 73728 | bytes 442368 | tf_op jit(solution)/shard_map/convert_element_type | solution.py:26
  9.6 0.0 all-gather.4.cloned.1.call-update
  9.6 1.4 %copy.11 = bf16[1,128,2304]{1,2,0:T(8,128)(2,1)S(1)} copy(bf16[1,128,2304]{2,1,0:T(8,128)(2,1)} %param.6) | data formatting | bytes 1179648 | tf_op args[0]
  11.0 28.6 %all_to_all.19 = bf16[128,16,144]{0,2,1:T(8,128)(2,1)S(1)} all-to-all(bf16[128,16,144]{0,2,1:T(8,128)(2,1)S(1)} %bitcast.62), channel_id=1, replica_groups=mesh['blk'=2,'fsdp'=16] {'fsdp'}, dimensions={1} | all-to-all | bytes 1179648 | tf_op jit(solution)/shard_map/all_to_all | solution.py:40
  39.6 0.0 copy-start.6
  39.6 0.0 copy-start.2
  39.6 18.2 %all-gather.6.cloned.1.call-done = bf16[1,2048,512]{2,1,0:T(8,128)(2,1)} async-done(((bf16[1,128,512]{2,1,0:T(8,128)(2,1)}), bf16[1,2048,512]{2,1,0:T(8,128)(2,1)}) %all-gather.6.cloned.1.call-update) | async-done | bytes 2097168 | tf_op jit(solution)/shard_map/all_gather | solution.py:44
  57.8 0.0 copy-done.3
  57.8 0.0 copy-done.4
  57.8 0.0 copy-done.5
  57.8 3.1 %fusion.18 = (bf16[144,512]{1,0:T(8,128)(2,1)S(1)}, f32[144,512]{1,0:T(8,128)S(1)}, f32[1,144,512]{2,1,0:T(8,128)}, f32[1,144,512]{2,1,0:T(8,128)}) fusion(f32[1,144,512]{2,1,0:T(8,128)S(1)} %copy-done.4, f32[1,144,512]{2,1,0:T(8,128)S(1)} %copy-done.5, f32[1,144,512]{2,1,0:T(8,128)S(1)} %copy-done.3, ...), kind=kOutput, calls=%fused_computation.27 | convolution fusion | flops 303243264 | bytes 4603904 | tf_op jit(solution)/shard_map/dot_general | solution.py:42
  60.9 0.0 copy-start.1
  60.9 1.5 %collective-permute-start = (bf16[144,512]{1,0:T(8,128)(2,1)S(1)}, bf16[144,512]{1,0:T(8,128)(2,1)S(1)}, u32[]{:S(2)}, u32[]{:S(2)}) collective-permute-start(bf16[144,512]{1,0:T(8,128)(2,1)S(1)} %get-tuple-element.5), channel_id=1, source_target_pairs={{0,16},{16,0},{1,17},{17,1},{2,18},{18,2},{3,19},{19,3},{4,20},{20... | collective-permute-start | bytes 442376 | tf_op jit(solution)/shard_map/ppermute | solution.py:19
  62.4 0.0 copy-done.6
  62.4 0.7 fusion.19
  64.9 1.9 %collective-permute-done = bf16[144,512]{1,0:T(8,128)(2,1)S(1)} collective-permute-done((bf16[144,512]{1,0:T(8,128)(2,1)S(1)}, bf16[144,512]{1,0:T(8,128)(2,1)S(1)}, u32[]{:S(2)}, u32[]{:S(2)}) %collective-permute-start) | collective-permute-done | bytes 147488 | tf_op jit(solution)/shard_map/ppermute | solution.py:19
  66.9 2.7 %fusion.12 = f32[1,144,512]{2,1,0:T(8,128)} fusion(bf16[144,512]{1,0:T(8,128)(2,1)S(1)} %collective-permute-done, f32[144,512]{1,0:T(8,128)S(1)} %get-tuple-element.6, f32[]{:T(128)S(6)} %add.35, f32[]{:T(128)} %bitcast.12, f32[]{:T(128)} %bitcast.11, f32[]{:T(128)} %bitcast.5), kind=kLoop, calls=%fused_computation.16 | loop fusion | flops 516096 | bytes 737296 | tf_op jit(solution)/shard_map/broadcast_in_dim | solution.py:65
  69.6 32.2 %all-gather.4.cloned.1.call-done = bf16[2304,512]{1,0:T(8,128)(2,1)} async-done(((bf16[144,512]{1,0:T(8,128)(2,1)}), bf16[2304,512]{1,0:T(8,128)(2,1)}) %all-gather.4.cloned.1.call-update) | async-done | bytes 2359312 | tf_op jit(solution)/shard_map/all_gather | solution.py:29
  101.7 0.0 copy-done.2
  101.7 0.0 copy-start
  101.7 3.5 %fusion.1 = bf16[1,128,2304]{2,1,0:T(8,128)(2,1)} fusion(bf16[2304,512]{1,0:T(8,128)(2,1)} %all-gather.4.cloned.1.call-done, bf16[1,128,512]{2,1,0:T(8,128)(2,1)S(1)} %copy-done.2), kind=kOutput, calls=%fused_computation.2 | convolution fusion | flops 302579712 | bytes 3080192 | tf_op jit(solution)/shard_map/dot_general | solution.py:33
  105.3 0.0 copy-done.1
  105.3 0.0 copy-done
  105.3 1.1 %fusion.5 = bf16[1,128,512]{2,1,0:T(8,128)(2,1)} fusion(bf16[2304,512]{1,0:T(8,128)(2,1)S(1)} %copy-done, bf16[1,128,2304]{2,1,0:T(8,128)(2,1)S(1)} %copy-done.1), kind=kOutput, calls=%fused_computation.7 | convolution fusion | flops 302120960 | bytes 3080192 | tf_op jit(solution)/shard_map/dot_general | solution.py:27
  (1 shorter events, 0.0 us)
Async XLA Ops:
  7.2 50.7 %copy-start.3 = (f32[1,144,512]{2,1,0:T(8,128)S(1)}, f32[1,144,512]{2,1,0:T(8,128)}, u32[]{:S(2)}) copy-start(f32[1,144,512]{2,1,0:T(8,128)} %param.8) | copy-start | bytes 884740
  7.2 50.6 %copy-start.4 = (f32[1,144,512]{2,1,0:T(8,128)S(1)}, f32[1,144,512]{2,1,0:T(8,128)}, u32[]{:S(2)}) copy-start(f32[1,144,512]{2,1,0:T(8,128)} %param.10) | copy-start | bytes 884740
  7.2 50.6 %copy-start.5 = (f32[1,144,512]{2,1,0:T(8,128)S(1)}, f32[1,144,512]{2,1,0:T(8,128)}, u32[]{:S(2)}) copy-start(f32[1,144,512]{2,1,0:T(8,128)} %param.9) | copy-start | bytes 884740
  7.2 50.6 %all-gather.6.cloned.1.call-start = ((), (), s32[]{:S(2)}) async-start(), calls=%async_computation.2 | async-start | bytes 2228224 | tf_op jit(solution)/shard_map/all_gather | solution.py:44
  7.9 93.8 %all-gather.4.cloned.1.call-start = ((), (), s32[]{:S(2)}) async-start(), calls=%async_computation.1 | async-start | bytes 2506752 | tf_op jit(solution)/shard_map/all_gather | solution.py:29
  39.6 22.7 %copy-start.6 = (s32[1,3]{1,0:T(1,128)S(1)}, s32[1,3]{1,0:T(1,128)}, u32[]{:S(2)}) copy-start(s32[1,3]{1,0:T(1,128)} %param.11) | copy-start | bytes 40
  39.6 62.1 %copy-start.2 = (bf16[1,128,512]{2,1,0:T(8,128)(2,1)S(1)}, bf16[1,128,512]{2,1,0:T(8,128)(2,1)}, u32[]{:S(2)}) copy-start(bf16[1,128,512]{2,1,0:T(8,128)(2,1)} %param.7) | copy-start | bytes 393220
  60.9 44.4 %copy-start.1 = (bf16[1,128,2304]{2,1,0:T(8,128)(2,1)S(1)}, bf16[1,128,2304]{2,1,0:T(8,128)(2,1)}, u32[]{:S(2)}) copy-start(bf16[1,128,2304]{2,1,0:T(8,128)(2,1)} %param.6) | copy-start | bytes 1769476
  60.9 6.0 %collective-permute-start = (bf16[144,512]{1,0:T(8,128)(2,1)S(1)}, bf16[144,512]{1,0:T(8,128)(2,1)S(1)}, u32[]{:S(2)}, u32[]{:S(2)}) collective-permute-start(bf16[144,512]{1,0:T(8,128)(2,1)S(1)} %get-tuple-element.5), channel_id=1, source_target_pairs={{0,16},{16,0},{1,17},{17,1},{2,18},{18,2},{3,19},{19,3},{4,20},{20... | collective-permute-start | bytes 442376 | tf_op jit(solution)/shard_map/ppermute | solution.py:19
  101.7 3.5 %copy-start = (bf16[2304,512]{1,0:T(8,128)(2,1)S(1)}, bf16[2304,512]{1,0:T(8,128)(2,1)}, u32[]{:S(2)}) copy-start(bf16[2304,512]{1,0:T(8,128)(2,1)} %all-gather.4.cloned.1.call-done) | copy-start | bytes 7077892
Sparse Core Ops, SparseCore 0:
  10.2 47.6 all-gather.5
  60.7 41.0 all-gather.3
where the time goes:
time: 114 us; the launch traced here: 113 us
  waiting for transfers between devices  53 us (46%)
  blocking collectives  28.6 us (25%)
  between operations  16 us (14%)
  matrix products  7.72 us (7%)
  other arithmetic  4.32 us (4%)
  local copies, waits for them, and re-layouts  2.05 us (2%)
  starting transfers between devices  1.55 us (1%)
    all_gather x1, waiting for transfers between devices, local(): lax.all_gather(compute_weights, 'fsdp', axis=0, tiled=True)  32.2 us
    all_to_all x1, blocking collectives, local(): lax.all_to_all(activations, 'fsdp', split_axis=1, concat_axis=0, tiled=True)  28.6 us
    all_gather x1, waiting for transfers between devices, local(): lax.all_gather(upstream, 'fsdp', axis=0, tiled=True)  18.2 us
    dot_general x1, matrix products, local(): lax.dot_general(upstream, lax.all_gather(compute_weights, 'fsdp', axis=0,...  3.51 us
    dot_general x1, matrix products, local(): lax.dot_general(owned_inputs, lax.all_gather(upstream, 'fsdp', axis=0, ti...  3.08 us
    broadcast_in_dim x1, other arithmetic, local(): averaged[None]  2.68 us
  transfers between devices with their start and end apart: 3, of which 3 were waited for; matrix products, arithmetic and copies ran while one was open for 8% of the time, Pallas kernels for 0%

commit v1 on v0

v1 whole, which is shorter than its diff:
```python
import functools
import math

import jax
import jax.numpy as jnp
from jax import lax
from jax.experimental import pallas as pl
from jax.experimental.pallas import tpu as pltpu
from jax.sharding import PartitionSpec as P

beta_one = 0.9
beta_two = 0.95
learn_rate = 0.05
weight_decay = 0.1
epsilon = 1e-08
correct_one = 1.0 - beta_one**5
correct_two = 1.0 - beta_two**5

BF = jnp.bfloat16
F32 = jnp.float32


def kernel(
    nz, nb, cut, factor,
    tok_h, cot_h, w_h, m1_h, m2_h, gos,
    key_o, ig_o, avg_o, m1_o, m2_o,
    w_v, m1_v, m2_v, tok2, cot2, wfull, part,
    xs_a, xr_a, zs_a, zr_a, zs_b, zr_b, xs_b, xr_b, ss, sr,
    load_sem, ce_s, ce_r, az_s, az_r, ax_s, ax_r, bx_s, bx_r, bz_s, bz_r,
    ca_s, ca_r, cb_s, cb_r, rax_s, rax_r, rza_s, rza_r, rzb_s, rzb_r, rbx_s, rbx_r, y_s, y_r,
):
    T, D = tok_h.shape
    R, H = w_h.shape
    me = lax.axis_index("fsdp")
    rep = lax.axis_index("blk")
    z = me // 4
    x = (me // 2) % 2
    c = me % 2
    low, high = cut, R - cut

    def dev(zz, xx, cc):
        return (rep, zz * 4 + xx * 2 + cc)

    def remote(src, dst, s, r, device):
        return pltpu.make_async_remote_copy(
            src_ref=src, dst_ref=dst, send_sem=s, recv_sem=r,
            device_id=device, device_id_type=pl.DeviceIdType.MESH,
        )

    loads = [
        pltpu.make_async_copy(w_h, w_v, load_sem.at[0]),
        pltpu.make_async_copy(cot_h, cot2.at[0:T], load_sem.at[1]),
        pltpu.make_async_copy(tok_h, tok2.at[0:T], load_sem.at[2]),
        pltpu.make_async_copy(m1_h, m1_v, load_sem.at[3]),
        pltpu.make_async_copy(m2_h, m2_v, load_sem.at[4]),
    ]
    for load in loads:
        load.start()

    barrier = pltpu.get_barrier_semaphore()

    def greet(device):
        pl.semaphore_signal(barrier, inc=1, device_id=device, device_id_type=pl.DeviceIdType.MESH)

    after = lax.rem(rep + 1, nb)
    before = lax.rem(rep + nb - 1, nb)
    x_dev = dev(z, 1 - x, c)
    c_dev = dev(z, x, 1 - c)
    greet(x_dev)
    greet(c_dev)
    greet((after, me))
    if nb > 2:
        greet((before, me))

    @pl.when(z > 0)
    def _():
        greet(dev(z - 1, x, c))

    @pl.when(z < nz - 1)
    def _():
        greet(dev(z + 1, x, c))

    loads[0].wait()
    wfull[z, x, c] = w_v[...].astype(BF)
    pl.semaphore_wait(barrier, (3 if nb > 2 else 2) + jnp.minimum(z, 1) + jnp.minimum(nz - 1 - z, 1) + (1 if nb > 1 else 0))

    ex_c = remote(cot_h, cot2.at[T : 2 * T], ce_s.at[0], ce_r.at[0], c_dev)
    ex_t = remote(tok_h, tok2.at[T : 2 * T], ce_s.at[1], ce_r.at[1], c_dev)
    ex_c.start()
    ex_t.start()

    def a_z(d, zz):
        ref = wfull.at[zz, x, c, 0:low]
        return remote(ref, ref, az_s.at[d, zz], az_r.at[zz], dev(z + 1 - 2 * d, x, c))

    def a_x(zz):
        ref = wfull.at[zz, x, c, 0:low]
        return remote(ref, ref, ax_s.at[zz], ax_r.at[zz], x_dev)

    def a_x_in(zz):
        ref = wfull.at[zz, 1 - x, c, 0:low]
        return remote(ref, ref, ax_s.at[zz], ax_r.at[zz], x_dev)

    own_b = wfull.at[z, x, c, low:R]
    b_x = remote(own_b, own_b, bx_s, bx_r, x_dev)

    def b_z(d, zz):
        ref = wfull.at[zz, :, c, low:R]
        return remote(ref, ref, bz_s.at[d, zz], bz_r.at[zz], dev(z + 1 - 2 * d, x, c))

    def core_a(zz, cc):
        ref = wfull.at[zz, :, cc, 0:low]
        return remote(ref, ref, ca_s.at[zz], ca_r.at[zz], c_dev)

    def core_b(zz, cc):
        ref = wfull.at[zz, :, cc, low:R]
        return remote(ref, ref, cb_s.at[zz], cb_r.at[zz], c_dev)

    b_x.start()

    @pl.when(z < nz - 1)
    def _():
        a_z(0, z).start()

    @pl.when(z > 0)
    def _():
        a_z(1, z).start()

    a_x(z).start()

    def gather_pair():
        b_x.wait_recv()

        @pl.when(z < nz - 1)
        def _():
            b_z(0, z).start()

        @pl.when(z > 0)
        def _():
            b_z(1, z).start()

        core_b(z, c).start()

    def gather_hop(k):
        for d in (0, 1):
            zz = z - k if d == 0 else z + k

            @pl.when((zz >= 0) & (zz < nz))
            def _():
                further = (z < nz - 1) if d == 0 else (z > 0)
                a_z(d, zz).wait_recv()

                @pl.when(further)
                def _():
                    a_z(d, zz).start()

                a_x(zz).start()
                b_z(d, zz).wait_recv()

                @pl.when(further)
                def _():
                    b_z(d, zz).start()

                core_b(zz, c).start()

    gather_pair()

    loads[1].wait()
    loads[2].wait()
    ex_c.wait_recv()
    ex_t.wait_recv()
    wide = math.gcd(D, 384)

    def partial(j, carry):
        at = pl.multiple_of(j * wide, wide)
        part[pl.ds(at, wide), :] = lax.dot_general(
            tok2[:, pl.ds(at, wide)], cot2[...], (((0,), (0,)), ((), ())), preferred_element_type=F32
        )
        return carry

    lax.fori_loop(0, D // wide, partial, 0)

    def mine(zz, xx, start, size):
        at = pl.multiple_of((zz * 4 + xx * 2 + c) * R + start, 16)
        return part[pl.ds(at, size), :]

    up_first = jnp.where(z >= nz // 2, 1, 0)

    def red_x(zz):
        return remote(xs_a.at[zz], xr_a.at[zz], rax_s.at[zz], rax_r.at[zz], x_dev)

    def send_a(k, carry):
        zz = (1 - up_first) * (nz - 1 - k) + up_first * k
        xs_a[zz] = mine(zz, 1 - x, 0, low).astype(BF)
        red_x(zz).start()
        return carry

    lax.fori_loop(0, nz, send_a, 0)

    def red_za(d, zz):
        return remote(zs_a.at[d, zz], zr_a.at[d, zz], rza_s.at[d, zz], rza_r.at[d, zz], dev(z + 1 - 2 * d, x, c))

    def red_zb(d, zz):
        return remote(zs_b.at[d, zz], zr_b.at[d, zz], rzb_s.at[d, zz], rzb_r.at[d, zz], dev(z + 1 - 2 * d, x, c))

    def chain(d, body):
        count = (1 - d) * (nz - 1 - z) + d * z
        fed = (1 - d) * z + d * (nz - 1 - z) > 0

        def step(k, carry):
            body((1 - d) * (nz - 1 - k) + d * k, fed)
            return carry

        lax.fori_loop(0, count, step, 0)

    def chain_a(d):
        def body(zz, fed):
            red_x(zz).wait_recv()
            base = mine(zz, x, 0, low) + xr_a[zz].astype(F32)

            @pl.when(fed)
            def _():
                red_za(d, zz).wait_recv()
                zs_a[d, zz] = (base + zr_a[d, zz].astype(F32)).astype(BF)

            @pl.when(jnp.logical_not(fed))
            def _():
                zs_a[d, zz] = base.astype(BF)

            red_za(d, zz).start()

        chain(d, body)

    def chain_b(d):
        def body(zz, fed):
            @pl.when(fed)
            def _():
                red_zb(d, zz).wait_recv()
                for xx in (0, 1):
                    zs_b[d, zz, xx] = (mine(zz, xx, low, high) + zr_b[d, zz, xx].astype(F32)).astype(BF)

            @pl.when(jnp.logical_not(fed))
            def _():
                for xx in (0, 1):
                    zs_b[d, zz, xx] = mine(zz, xx, low, high).astype(BF)

            red_zb(d, zz).start()

        chain(d, body)

    gather_hop(1)
    chain_b(up_first)
    if nz > 2:
        gather_hop(2)
    chain_b(1 - up_first)
    chain_a(up_first)
    for k in range(3, nz):
        gather_hop(k)
    chain_a(1 - up_first)

    def own_at(xx, start):
        return pl.ds(pl.multiple_of((z * 4 + xx * 2 + c) * R + start, 16), low if start == 0 else high)

    for d in (0, 1):
        @pl.when((z > 0) if d == 0 else (z < nz - 1))
        def _():
            red_zb(d, z).wait_recv()
            for xx in (0, 1):
                part[own_at(xx, low), :] += zr_b[d, z, xx].astype(F32)

    red_bx = remote(xs_b, xr_b, rbx_s, rbx_r, x_dev)
    xs_b[...] = mine(z, 1 - x, low, high).astype(BF)
    red_bx.start()
    red_x(z).wait_recv()
    part[own_at(x, 0), :] += xr_a[z].astype(F32)
    for d in (0, 1):
        @pl.when((z > 0) if d == 0 else (z < nz - 1))
        def _():
            red_za(d, z).wait_recv()
            part[own_at(x, 0), :] += zr_a[d, z].astype(F32)

    loads[3].wait()
    loads[4].wait()
    red_bx.wait_recv()
    part[own_at(x, low), :] += xr_b[...].astype(F32)

    gradient = part[pl.ds(pl.multiple_of(me * R, 16), R), :] * factor
    new_one = beta_one * m1_v[...] + (1.0 - beta_one) * gradient
    new_two = beta_two * m2_v[...] + (1.0 - beta_two) * gradient * gradient
    m1_o[...] = new_one
    m2_o[...] = new_two
    update = new_one / correct_one / (jnp.sqrt(new_two / correct_two) + epsilon)
    master = w_v[...]
    stepped = master - learn_rate * (update + weight_decay * master)
    w_v[...] = stepped
    ss[...] = stepped.astype(BF)
    ys = [remote(ss, sr.at[0], y_s.at[0], y_r.at[0], (after, me))]
    if nb > 2:
        ys.append(remote(ss, sr.at[1], y_s.at[1], y_r.at[1], (before, me)))
    for y in ys:
        y.start()

    for zz in range(nz):
        a_x_in(zz).wait_recv()
        core_a(zz, c).start()
    group = 1
    while (group * 4 * R) % 128:
        group += 1
    rows = group * 4 * R
    tokens = tok2[0:T, :]
    upstream = cot2[0:T, :]
    total = jnp.zeros((T, H), F32)
    for first in range(0, nz, group):
        for zz in range(first, first + group):
            core_a(zz, 1 - c).wait_recv()
            core_b(zz, 1 - c).wait_recv()
        block = wfull[first : first + group].reshape(rows, H)
        span = slice(first * 4 * R, first * 4 * R + rows)
        total += jnp.dot(tokens[:, span], block, preferred_element_type=F32)
        ig_o[:, span] = (
            lax.dot_general(upstream, block, (((1,), (1,)), ((), ())), preferred_element_type=F32) * factor
        ).astype(BF)
    key_o[...] = (total * factor).astype(BF)

    left = gos[0, 0].astype(F32)
    self_ = gos[0, 1].astype(F32)
    right = gos[0, 2].astype(F32)
    for y in ys:
        y.wait_recv()
    from_before = sr[0].astype(F32)
    from_after = sr[1].astype(F32) if nb > 2 else from_before
    weight = jnp.full((R, H), left + self_ + right, F32)
    avg_o[...] = (left * from_before + self_ * w_v[...] + right * from_after) / weight

    ex_c.wait_send()
    ex_t.wait_send()
    b_x.wait_send()
    for y in ys:
        y.wait_send()
    red_bx.wait_send()
    for zz in range(nz):
        a_x(zz).wait_send()
        core_a(zz, c).wait_send()
        core_b(zz, c).wait_send()
        red_x(zz).wait_send()
        for d in (0, 1):
            from_here = (zz <= z) & (z < nz - 1) if d == 0 else (zz >= z) & (z > 0)

            @pl.when(from_here)
            def _():
                a_z(d, zz).wait_send()
                b_z(d, zz).wait_send()

            @pl.when((zz > z) if d == 0 else (zz < z))
            def _():
                red_za(d, zz).wait_send()
                red_zb(d, zz).wait_send()


def local(nz, nb, tokens, cotangent, weights, moment_one, moment_two, gossip):
    _, T, D = tokens.shape
    _, R, H = weights.shape
    n = nz * 4
    factor = 1.0 / math.sqrt(D)
    cut = 16 * max(1, round(R / 16 * 5 / 9))
    high = R - cut
    dma = pltpu.SemaphoreType.DMA
    vmem = pl.BlockSpec(memory_space=pltpu.VMEM)
    hbm = pl.BlockSpec(memory_space=pl.ANY)
    outs = pl.pallas_call(
        functools.partial(kernel, nz, nb, cut, factor),
        out_shape=(
            jax.ShapeDtypeStruct((T, H), BF),
            jax.ShapeDtypeStruct((T, D), BF),
            jax.ShapeDtypeStruct((R, H), F32),
            jax.ShapeDtypeStruct((R, H), F32),
            jax.ShapeDtypeStruct((R, H), F32),
        ),
        in_specs=[hbm] * 5 + [pl.BlockSpec(memory_space=pltpu.SMEM)],
        out_specs=(vmem,) * 5,
        scratch_shapes=[
            pltpu.VMEM((R, H), F32),
            pltpu.VMEM((R, H), F32),
            pltpu.VMEM((R, H), F32),
            pltpu.VMEM((2 * T, D), BF),
            pltpu.VMEM((2 * T, H), BF),
            pltpu.VMEM((nz, 2, 2, R, H), BF),
            pltpu.VMEM((D, H), F32),
            pltpu.VMEM((nz, cut, H), BF),
            pltpu.VMEM((nz, cut, H), BF),
            pltpu.VMEM((2, nz, cut, H), BF),
            pltpu.VMEM((2, nz, cut, H), BF),
            pltpu.VMEM((2, nz, 2, high, H), BF),
            pltpu.VMEM((2, nz, 2, high, H), BF),
            pltpu.VMEM((high, H), BF),
            pltpu.VMEM((high, H), BF),
            pltpu.VMEM((R, H), BF),
            pltpu.VMEM((2, R, H), BF),
            dma((5,)),
            dma((2,)), dma((2,)),
            dma((2, nz)), dma((nz,)),
            dma((nz,)), dma((nz,)),
            dma, dma,
            dma((2, nz)), dma((nz,)),
            dma((nz,)), dma((nz,)),
            dma((nz,)), dma((nz,)),
            dma((nz,)), dma((nz,)),
            dma((2, nz)), dma((2, nz)),
            dma((2, nz)), dma((2, nz)),
            dma, dma,
            dma((2,)), dma((2,)),
        ],
        compiler_params=pltpu.CompilerParams(
            collective_id=0, has_side_effects=True, vmem_limit_bytes=48 * 1024 * 1024
        ),
        name="step",
    )(tokens[0], cotangent[0], weights[0], moment_one[0], moment_two[0], gossip)
    return tuple(out[None] for out in outs)


def solution(mesh):
    wide = P("blk", "fsdp", None)
    nz = mesh.shape["fsdp"] // 4
    return jax.shard_map(
        functools.partial(local, nz, mesh.shape["blk"]),
        mesh=mesh,
        in_specs=(wide,) * 5 + (P("blk", None),),
        out_specs=(wide,) * 5,
        check_vma=False,
    )
```

time: 114 us -> 48.4 us (0.42)
  waiting for transfers between devices: 53 us -> 0 us
  Pallas kernels: 0 us -> 38.4 us
  blocking collectives: 28.6 us -> 0 us
  between operations: 16 us -> 0.66 us
  matrix products: 7.72 us -> 0 us
  local copies, waits for them, and re-layouts: 2.05 us -> 9.11 us
  other arithmetic: 4.32 us -> 0 us
  starting transfers between devices: 1.55 us -> 0 us
    all_gather x2 -> x0, waiting for transfers between devices: 50.3 us -> none  [the longest x1 32.2 us: local(): lax.all_gather(compute_weights, 'fsdp', axis=0, tiled=True)]
    pallas_call x0 -> x1, Pallas kernels: none -> 38.4 us  [local(): pl.pallas_call(functools.partial(kernel, nz, nb, cut, factor), out_shape=...]
    all_to_all x1 -> x0, blocking collectives: 28.6 us -> none  [local(): lax.all_to_all(activations, 'fsdp', split_axis=1, concat_axis=0, tiled=True)]
    unnamed x15 -> x17, local copies, waits for them, and re-layouts: 1.39 us -> 9.11 us
    dot_general x3 -> x0, matrix products: 7.72 us -> none  [the longest x1 3.51 us: local(): lax.dot_general(upstream, lax.all_gather(compute_weights, 'fsdp', axis=0,...]
    broadcast_in_dim x1 -> x0, other arithmetic: 2.68 us -> none  [local(): averaged[None]]
    ppermute x1 -> x0, waiting for transfers between devices: 1.94 us -> none  [from_behind(): lax.ppermute(shard, axis, [(i, (i + by) % length) for i in range(length)])]
    convert_element_type x2 -> x0, other arithmetic: 1.64 us -> none  [the longest x1 1.64 us: local(): compute_weights = weights[0].astype(jnp.bfloat16)]
  transfers between devices with their start and end apart: 3 -> 0, of which waited for: 3 -> 0; matrix products, arithmetic and copies ran while one was open for 8% -> 0% of each run, Pallas kernels for 0% -> 0%
where the time goes in v1:
time: 48.4 us; the launch traced here: 48.1 us
  Pallas kernels  38.4 us (79%)
  local copies, waits for them, and re-layouts  9.11 us (19%)
  between operations  0.66 us (1%)
    pallas_call x1, Pallas kernels, local(): pl.pallas_call(functools.partial(kernel, nz, nb, cut, factor), out_shape=...  38.4 us
    unnamed x17, local copies, waits for them, and re-layouts  9.11 us

profile of v1, /device:TPU:0, one launch (start us, length us, event | category | flops | bytes accessed | tf_op | source)
XLA Modules:
  0.0 48.1 jit_solution(17363957627312330376)
XLA Ops:
  0.6 0.0 copy-start.5
  0.6 0.6 %copy-done.5 = s32[1,3]{1,0:T(1,128)S(1)} copy-done((s32[1,3]{1,0:T(1,128)S(1)}, s32[1,3]{1,0:T(1,128)}, u32[]{:S(2)}) %copy-start.5) | copy-done | bytes 36
  1.3 0.0 copy-start
  1.3 1.1 %copy-done = bf16[1,128,2304]{2,1,0:T(8,128)(2,1)S(1)} copy-done((bf16[1,128,2304]{2,1,0:T(8,128)(2,1)S(1)}, bf16[1,128,2304]{2,1,0:T(8,128)(2,1)}, u32[]{:S(2)}) %copy-start) | copy-done | bytes 589848
  2.4 0.0 copy-start.1
  2.4 1.0 %copy-done.1 = f32[1,144,512]{2,1,0:T(8,128)S(1)} copy-done((f32[1,144,512]{2,1,0:T(8,128)S(1)}, f32[1,144,512]{2,1,0:T(8,128)}, u32[]{:S(2)}) %copy-start.1) | copy-done | bytes 294936
  3.3 0.0 copy-start.2
  3.3 1.0 %copy-done.2 = f32[1,144,512]{2,1,0:T(8,128)S(1)} copy-done((f32[1,144,512]{2,1,0:T(8,128)S(1)}, f32[1,144,512]{2,1,0:T(8,128)}, u32[]{:S(2)}) %copy-start.2) | copy-done | bytes 294936
  4.3 0.0 copy-start.3
  4.3 1.0 %copy-done.3 = f32[1,144,512]{2,1,0:T(8,128)S(1)} copy-done((f32[1,144,512]{2,1,0:T(8,128)S(1)}, f32[1,144,512]{2,1,0:T(8,128)}, u32[]{:S(2)}) %copy-start.3) | copy-done | bytes 294936
  5.2 0.0 copy-start.4
  5.2 0.9 %copy-done.4 = bf16[1,128,512]{2,1,0:T(8,128)(2,1)S(1)} copy-done((bf16[1,128,512]{2,1,0:T(8,128)(2,1)S(1)}, bf16[1,128,512]{2,1,0:T(8,128)(2,1)}, u32[]{:S(2)}) %copy-start.4) | copy-done | bytes 131096
  6.1 38.4 %step.1 = (bf16[128,512]{1,0:T(8,128)(2,1)S(1)}, bf16[128,2304]{1,0:T(8,128)(2,1)S(1)}, f32[144,512]{1,0:T(8,128)S(1)}, f32[144,512]{1,0:T(8,128)S(1)}, f32[144,512]{1,0:T(8,128)S(1)}) custom-call(bf16[128,2304]{1,0:T(8,128)(2,1)S(1)} %bitcast.10, bf16[128,512]{1,0:T(8,128)(2,1)S(1)} %bitcast.18, f32[144,512]{1,0:T(8,128)S(1)} %bitcast.15, ...), custom_call_target="tpu_custom_call" | custom-call | tf_op jit(solution)/shard_map/step/pallas_call | solution.py:370
  44.5 0.7 %copy.16 = bf16[1,128,512]{2,1,0:T(8,128)(2,1)} copy(bf16[1,128,512]{2,1,0:T(8,128)(2,1)S(1)} %bitcast.19) | data formatting | bytes 262144
  45.2 0.8 %copy.17 = bf16[1,128,2304]{2,1,0:T(8,128)(2,1)} copy(bf16[1,128,2304]{2,1,0:T(8,128)(2,1)S(1)} %bitcast.11) | data formatting | bytes 1179648
  46.0 0.7 %copy.18 = f32[1,144,512]{2,1,0:T(8,128)} copy(f32[1,144,512]{2,1,0:T(8,128)S(1)} %bitcast.14) | data formatting | bytes 589824
  46.7 0.7 %copy.19 = f32[1,144,512]{2,1,0:T(8,128)} copy(f32[1,144,512]{2,1,0:T(8,128)S(1)} %bitcast.13) | data formatting | bytes 589824
  47.4 0.7 %copy.20 = f32[1,144,512]{2,1,0:T(8,128)} copy(f32[1,144,512]{2,1,0:T(8,128)S(1)} %bitcast.12) | data formatting | bytes 589824
Async XLA Ops:
  0.6 0.7 %copy-start.5 = (s32[1,3]{1,0:T(1,128)S(1)}, s32[1,3]{1,0:T(1,128)}, u32[]{:S(2)}) copy-start(s32[1,3]{1,0:T(1,128)} %gos.1) | copy-start | bytes 40
  1.3 1.1 %copy-start = (bf16[1,128,2304]{2,1,0:T(8,128)(2,1)S(1)}, bf16[1,128,2304]{2,1,0:T(8,128)(2,1)}, u32[]{:S(2)}) copy-start(bf16[1,128,2304]{2,1,0:T(8,128)(2,1)} %param.6) | copy-start | bytes 1769476
  2.4 1.0 %copy-start.1 = (f32[1,144,512]{2,1,0:T(8,128)S(1)}, f32[1,144,512]{2,1,0:T(8,128)}, u32[]{:S(2)}) copy-start(f32[1,144,512]{2,1,0:T(8,128)} %param.8) | copy-start | bytes 884740
  3.3 1.0 %copy-start.2 = (f32[1,144,512]{2,1,0:T(8,128)S(1)}, f32[1,144,512]{2,1,0:T(8,128)}, u32[]{:S(2)}) copy-start(f32[1,144,512]{2,1,0:T(8,128)} %param.9) | copy-start | bytes 884740
  4.3 1.0 %copy-start.3 = (f32[1,144,512]{2,1,0:T(8,128)S(1)}, f32[1,144,512]{2,1,0:T(8,128)}, u32[]{:S(2)}) copy-start(f32[1,144,512]{2,1,0:T(8,128)} %param.10) | copy-start | bytes 884740
  5.2 0.9 %copy-start.4 = (bf16[1,128,512]{2,1,0:T(8,128)(2,1)S(1)}, bf16[1,128,512]{2,1,0:T(8,128)(2,1)}, u32[]{:S(2)}) copy-start(bf16[1,128,512]{2,1,0:T(8,128)(2,1)} %param.7) | copy-start | bytes 393220

commit v2 on v1

--- a/solution.py
+++ b/solution.py
@@ -22,9 +22,9 @@
 
 def kernel(
     nz, nb, cut, factor,
-    tok_h, cot_h, w_h, m1_h, m2_h, gos,
+    tok_h, cot_h, w_h, m1_h, m2_h, gos_h,
     key_o, ig_o, avg_o, m1_o, m2_o,
-    w_v, m1_v, m2_v, tok2, cot2, wfull, part,
+    gos, w_v, m1_v, m2_v, tok2, cot2, wfull, part,
     xs_a, xr_a, zs_a, zr_a, zs_b, zr_b, xs_b, xr_b, ss, sr,
     load_sem, ce_s, ce_r, az_s, az_r, ax_s, ax_r, bx_s, bx_r, bz_s, bz_r,
     ca_s, ca_r, cb_s, cb_r, rax_s, rax_r, rza_s, rza_r, rzb_s, rzb_r, rbx_s, rbx_r, y_s, y_r,
@@ -53,6 +53,7 @@
         pltpu.make_async_copy(tok_h, tok2.at[0:T], load_sem.at[2]),
         pltpu.make_async_copy(m1_h, m1_v, load_sem.at[3]),
         pltpu.make_async_copy(m2_h, m2_v, load_sem.at[4]),
+        pltpu.make_async_copy(gos_h, gos, load_sem.at[5]),
     ]
     for load in loads:
         load.start()
@@ -248,15 +249,27 @@
 
         chain(d, body)
 
-    gather_hop(1)
-    chain_b(up_first)
-    if nz > 2:
-        gather_hop(2)
-    chain_b(1 - up_first)
-    chain_a(up_first)
-    for k in range(3, nz):
-        gather_hop(k)
-    chain_a(1 - up_first)
+    at_end = (z == 0) | (z == nz - 1)
+
+    @pl.when(at_end)
+    def _():
+        chain_b(up_first)
+        gather_hop(1)
+        chain_a(up_first)
+        for k in range(2, nz):
+            gather_hop(k)
+
+    @pl.when(jnp.logical_not(at_end))
+    def _():
+        gather_hop(1)
+        chain_b(up_first)
+        if nz > 2:
+            gather_hop(2)
+        chain_b(1 - up_first)
+        chain_a(up_first)
+        for k in range(3, nz):
+            gather_hop(k)
+        chain_a(1 - up_first)
 
     def own_at(xx, start):
         return pl.ds(pl.multiple_of((z * 4 + xx * 2 + c) * R + start, 16), low if start == 0 else high)
@@ -281,24 +294,38 @@
 
     loads[3].wait()
     loads[4].wait()
+
+    def to(peer, side, index, start, size):
+        return remote(
+            ss.at[start : start + size], sr.at[side, start : start + size],
+            y_s.at[side, index], y_r.at[side, index], (peer, me),
+        )
+
+    ys = []
+
+    def optimize(index, start, size):
+        span = slice(start, start + size)
+        gradient = part[own_at(x, start), :] * factor
+        new_one = beta_one * m1_v[span] + (1.0 - beta_one) * gradient
+        new_two = beta_two * m2_v[span] + (1.0 - beta_two) * gradient * gradient
+        m1_o[span] = new_one
+        m2_o[span] = new_two
+        update = new_one / correct_one / (jnp.sqrt(new_two / correct_two) + epsilon)
+        master = w_v[span]
+        stepped = master - learn_rate * (update + weight_decay * master)
+        w_v[span] = stepped
+        ss[span] = stepped.astype(BF)
+        pair = [to(after, 0, index, start, size)]
+        if nb > 2:
+            pair.append(to(before, 1, index, start, size))
+        for y in pair:
+            y.start()
+        ys.extend(pair)
+
+    optimize(0, 0, low)
     red_bx.wait_recv()
     part[own_at(x, low), :] += xr_b[...].astype(F32)
-
-    gradient = part[pl.ds(pl.multiple_of(me * R, 16), R), :] * factor
-    new_one = beta_one * m1_v[...] + (1.0 - beta_one) * gradient
-    new_two = beta_two * m2_v[...] + (1.0 - beta_two) * gradient * gradient
-    m1_o[...] = new_one
-    m2_o[...] = new_two
-    update = new_one / correct_one / (jnp.sqrt(new_two / correct_two) + epsilon)
-    master = w_v[...]
-    stepped = master - learn_rate * (update + weight_decay * master)
-    w_v[...] = stepped
-    ss[...] = stepped.astype(BF)
-    ys = [remote(ss, sr.at[0], y_s.at[0], y_r.at[0], (after, me))]
-    if nb > 2:
-        ys.append(remote(ss, sr.at[1], y_s.at[1], y_r.at[1], (before, me)))
-    for y in ys:
-        y.start()
+    optimize(1, low, high)
 
     for zz in range(nz):
         a_x_in(zz).wait_recv()
@@ -322,6 +349,7 @@
         ).astype(BF)
     key_o[...] = (total * factor).astype(BF)
 
+    loads[5].wait()
     left = gos[0, 0].astype(F32)
     self_ = gos[0, 1].astype(F32)
     right = gos[0, 2].astype(F32)
@@ -355,6 +383,15 @@
             def _():
                 red_za(d, zz).wait_send()
                 red_zb(d, zz).wait_send()
+
+
+def put_out(*refs):
+    ins, outs, sem = refs[:5], refs[5:10], refs[10]
+    copies = [pltpu.make_async_copy(a, b, sem.at[i]) for i, (a, b) in enumerate(zip(ins, outs))]
+    for copy in copies:
+        copy.start()
+    for copy in copies:
+        copy.wait()
 
 
 def local(nz, nb, tokens, cotangent, weights, moment_one, moment_two, gossip):
@@ -376,9 +413,10 @@
             jax.ShapeDtypeStruct((R, H), F32),
             jax.ShapeDtypeStruct((R, H), F32),
         ),
-        in_specs=[hbm] * 5 + [pl.BlockSpec(memory_space=pltpu.SMEM)],
+        in_specs=[hbm] * 6,
         out_specs=(vmem,) * 5,
         scratch_shapes=[
+            pltpu.SMEM(gossip.shape, gossip.dtype),
             pltpu.VMEM((R, H), F32),
             pltpu.VMEM((R, H), F32),
             pltpu.VMEM((R, H), F32),
@@ -396,7 +434,7 @@
             pltpu.VMEM((high, H), BF),
             pltpu.VMEM((R, H), BF),
             pltpu.VMEM((2, R, H), BF),
-            dma((5,)),
+            dma((6,)),
             dma((2,)), dma((2,)),
             dma((2, nz)), dma((nz,)),
             dma((nz,)), dma((nz,)),
@@ -408,13 +446,21 @@
             dma((2, nz)), dma((2, nz)),
             dma((2, nz)), dma((2, nz)),
             dma, dma,
-            dma((2,)), dma((2,)),
+            dma((2, 2)), dma((2, 2)),
         ],
         compiler_params=pltpu.CompilerParams(
-            collective_id=0, has_side_effects=True, vmem_limit_bytes=48 * 1024 * 1024
+            collective_id=0, has_side_effects=True
         ),
         name="step",
     )(tokens[0], cotangent[0], weights[0], moment_one[0], moment_two[0], gossip)
+    outs = pl.pallas_call(
+        put_out,
+        out_shape=tuple(jax.ShapeDtypeStruct(out.shape, out.dtype) for out in outs),
+        in_specs=[vmem] * 5,
+        out_specs=(hbm,) * 5,
+        scratch_shapes=[dma((5,))],
+        name="put_out",
+    )(*outs)
     return tuple(out[None] for out in outs)
 
 

time: 48.4 us -> 41.5 us (0.86)
  local copies, waits for them, and re-layouts: 9.11 us -> 0 us
  Pallas kernels: 38.4 us -> 40.7 us
    unnamed x17 -> x0, local copies, waits for them, and re-layouts: 9.11 us -> none
    pallas_call x0 -> x1, Pallas kernels: none -> 2.55 us  [local(): pl.pallas_call(put_out, out_shape=tuple((jax.ShapeDtypeStruct(out.shape,...]
where the time goes in v2:
time: 41.5 us; the launch traced here: 41.4 us
  Pallas kernels  40.7 us (98%)
  between operations  0.64 us (2%)
    pallas_call x1, Pallas kernels, local(): pl.pallas_call(functools.partial(kernel, nz, nb, cut, factor), out_shape=...  38.2 us
    pallas_call x1, Pallas kernels, local(): pl.pallas_call(put_out, out_shape=tuple((jax.ShapeDtypeStruct(out.shape,...  2.55 us

profile of v2, /device:TPU:0, one launch (start us, length us, event | category | flops | bytes accessed | tf_op | source)
XLA Modules:
  0.0 41.4 jit_solution(16397934595149386784)
XLA Ops:
  0.6 38.2 %step.1 = (bf16[128,512]{1,0:T(8,128)(2,1)}, bf16[128,2304]{1,0:T(8,128)(2,1)}, f32[144,512]{1,0:T(8,128)}, f32[144,512]{1,0:T(8,128)}, f32[144,512]{1,0:T(8,128)}) custom-call(bf16[128,2304]{1,0:T(8,128)(2,1)} %bitcast.10, bf16[128,512]{1,0:T(8,128)(2,1)} %bitcast.14, f32[144,512]{1,0:T(8,128)} %bitcast.11, f32[144,512]{1,0:T(8,128)} %bitcast.12, ...), custom_call_target="tpu_custom_call" | custom-call | tf_op jit(solution)/shard_map/step/pallas_call | solution.py:407
  38.8 2.5 %put_out.1 = (bf16[128,512]{1,0:T(8,128)(2,1)}, bf16[128,2304]{1,0:T(8,128)(2,1)}, f32[144,512]{1,0:T(8,128)}, f32[144,512]{1,0:T(8,128)}, f32[144,512]{1,0:T(8,128)}) custom-call(bf16[128,512]{1,0:T(8,128)(2,1)} %get-tuple-element.15.refs_0_, bf16[128,2304]{1,0:T(8,128)(2,1)} %get-tuple-element.16.refs_1_, f32[144,512]{1,0:T(8,128)} %get-tuple-element.17.refs_2_, ...), custom_call_target="tpu_custom_call" | custom-call | tf_op jit(solution)/shard_map/put_out/pallas_call | solution.py:456

commit v3 on v2

--- a/solution.py
+++ b/solution.py
@@ -21,7 +21,7 @@
 
 
 def kernel(
-    nz, nb, cut, factor,
+    nz, nb, keep, cut, factor,
     tok_h, cot_h, w_h, m1_h, m2_h, gos_h,
     key_o, ig_o, avg_o, m1_o, m2_o,
     gos, w_v, m1_v, m2_v, tok2, cot2, wfull, part,
@@ -73,17 +73,14 @@
     if nb > 2:
         greet((before, me))
 
-    @pl.when(z > 0)
-    def _():
-        greet(dev(z - 1, x, c))
-
-    @pl.when(z < nz - 1)
-    def _():
-        greet(dev(z + 1, x, c))
-
+    def greet_column(k, carry):
+        greet(dev(lax.rem(z + k, nz), x, c))
+        return carry
+
+    lax.fori_loop(1, nz, greet_column, 0)
     loads[0].wait()
     wfull[z, x, c] = w_v[...].astype(BF)
-    pl.semaphore_wait(barrier, (3 if nb > 2 else 2) + jnp.minimum(z, 1) + jnp.minimum(nz - 1 - z, 1) + (1 if nb > 1 else 0))
+    pl.semaphore_wait(barrier, (4 if nb > 2 else 3) + nz - 1)
 
     ex_c = remote(cot_h, cot2.at[T : 2 * T], ce_s.at[0], ce_r.at[0], c_dev)
     ex_t = remote(tok_h, tok2.at[T : 2 * T], ce_s.at[1], ce_r.at[1], c_dev)
@@ -91,30 +88,30 @@
     ex_t.start()
 
     def a_z(d, zz):
-        ref = wfull.at[zz, x, c, 0:low]
+        ref = wfull.at[zz, x, c, 0:keep]
         return remote(ref, ref, az_s.at[d, zz], az_r.at[zz], dev(z + 1 - 2 * d, x, c))
 
     def a_x(zz):
-        ref = wfull.at[zz, x, c, 0:low]
+        ref = wfull.at[zz, x, c, 0:keep]
         return remote(ref, ref, ax_s.at[zz], ax_r.at[zz], x_dev)
 
     def a_x_in(zz):
-        ref = wfull.at[zz, 1 - x, c, 0:low]
+        ref = wfull.at[zz, 1 - x, c, 0:keep]
         return remote(ref, ref, ax_s.at[zz], ax_r.at[zz], x_dev)
 
-    own_b = wfull.at[z, x, c, low:R]
+    own_b = wfull.at[z, x, c, keep:R]
     b_x = remote(own_b, own_b, bx_s, bx_r, x_dev)
 
     def b_z(d, zz):
-        ref = wfull.at[zz, :, c, low:R]
+        ref = wfull.at[zz, :, c, keep:R]
         return remote(ref, ref, bz_s.at[d, zz], bz_r.at[zz], dev(z + 1 - 2 * d, x, c))
 
     def core_a(zz, cc):
-        ref = wfull.at[zz, :, cc, 0:low]
+        ref = wfull.at[zz, :, cc, 0:keep]
         return remote(ref, ref, ca_s.at[zz], ca_r.at[zz], c_dev)
 
     def core_b(zz, cc):
-        ref = wfull.at[zz, :, cc, low:R]
+        ref = wfull.at[zz, :, cc, keep:R]
         return remote(ref, ref, cb_s.at[zz], cb_r.at[zz], c_dev)
 
     b_x.start()
@@ -170,128 +167,86 @@
     loads[2].wait()
     ex_c.wait_recv()
     ex_t.wait_recv()
-    wide = math.gcd(D, 384)
-
-    def partial(j, carry):
-        at = pl.multiple_of(j * wide, wide)
-        part[pl.ds(at, wide), :] = lax.dot_general(
-            tok2[:, pl.ds(at, wide)], cot2[...], (((0,), (0,)), ((), ())), preferred_element_type=F32
-        )
-        return carry
-
-    lax.fori_loop(0, D // wide, partial, 0)
+    group = 1
+    while (group * 4 * R) % 128:
+        group += 1
+    rows = group * 4 * R
+    wide = math.gcd(rows, 384)
 
     def mine(zz, xx, start, size):
         at = pl.multiple_of((zz * 4 + xx * 2 + c) * R + start, 16)
         return part[pl.ds(at, size), :]
 
-    up_first = jnp.where(z >= nz // 2, 1, 0)
-
     def red_x(zz):
         return remote(xs_a.at[zz], xr_a.at[zz], rax_s.at[zz], rax_r.at[zz], x_dev)
 
-    def send_a(k, carry):
-        zz = (1 - up_first) * (nz - 1 - k) + up_first * k
+    def red_za(zz, source):
+        return remote(zs_a.at[zz], zr_a.at[source], rza_s.at[zz], rza_r.at[source], dev(zz, x, c))
+
+    def red_zb(zz, source):
+        return remote(zs_b.at[zz], zr_b.at[source], rzb_s.at[zz], rzb_r.at[source], dev(zz, x, c))
+
+    def first_sends(zz):
+        @pl.when(zz != z)
+        def _():
+            for xx in (0, 1):
+                zs_b[zz, xx] = mine(zz, xx, low, high).astype(BF)
+            red_zb(zz, z).start()
+
         xs_a[zz] = mine(zz, 1 - x, 0, low).astype(BF)
         red_x(zz).start()
-        return carry
-
-    lax.fori_loop(0, nz, send_a, 0)
-
-    def red_za(d, zz):
-        return remote(zs_a.at[d, zz], zr_a.at[d, zz], rza_s.at[d, zz], rza_r.at[d, zz], dev(z + 1 - 2 * d, x, c))
-
-    def red_zb(d, zz):
-        return remote(zs_b.at[d, zz], zr_b.at[d, zz], rzb_s.at[d, zz], rzb_r.at[d, zz], dev(z + 1 - 2 * d, x, c))
-
-    def chain(d, body):
-        count = (1 - d) * (nz - 1 - z) + d * z
-        fed = (1 - d) * z + d * (nz - 1 - z) > 0
-
-        def step(k, carry):
-            body((1 - d) * (nz - 1 - k) + d * k, fed)
-            return carry
-
-        lax.fori_loop(0, count, step, 0)
-
-    def chain_a(d):
-        def body(zz, fed):
+
+    def second_sends(zz):
+        @pl.when(zz != z)
+        def _():
             red_x(zz).wait_recv()
-            base = mine(zz, x, 0, low) + xr_a[zz].astype(F32)
-
-            @pl.when(fed)
-            def _():
-                red_za(d, zz).wait_recv()
-                zs_a[d, zz] = (base + zr_a[d, zz].astype(F32)).astype(BF)
-
-            @pl.when(jnp.logical_not(fed))
-            def _():
-                zs_a[d, zz] = base.astype(BF)
-
-            red_za(d, zz).start()
-
-        chain(d, body)
-
-    def chain_b(d):
-        def body(zz, fed):
-            @pl.when(fed)
-            def _():
-                red_zb(d, zz).wait_recv()
-                for xx in (0, 1):
-                    zs_b[d, zz, xx] = (mine(zz, xx, low, high) + zr_b[d, zz, xx].astype(F32)).astype(BF)
-
-            @pl.when(jnp.logical_not(fed))
-            def _():
-                for xx in (0, 1):
-                    zs_b[d, zz, xx] = mine(zz, xx, low, high).astype(BF)
-
-            red_zb(d, zz).start()
-
-        chain(d, body)
-
-    at_end = (z == 0) | (z == nz - 1)
-
-    @pl.when(at_end)
-    def _():
-        chain_b(up_first)
-        gather_hop(1)
-        chain_a(up_first)
-        for k in range(2, nz):
-            gather_hop(k)
-
-    @pl.when(jnp.logical_not(at_end))
-    def _():
-        gather_hop(1)
-        chain_b(up_first)
-        if nz > 2:
-            gather_hop(2)
-        chain_b(1 - up_first)
-        chain_a(up_first)
-        for k in range(3, nz):
-            gather_hop(k)
-        chain_a(1 - up_first)
+            zs_a[zz] = (mine(zz, x, 0, low) + xr_a[zz].astype(F32)).astype(BF)
+            red_za(zz, z).start()
+
+    def ordered(step, k):
+        slot = lax.rem(z // group + 1 + k // group, nz // group)
+        step(slot * group + k % group)
+
+    for k in range(0, nz, group):
+        base = lax.rem(z // group + 1 + k // group, nz // group) * rows
+        for j in range(rows // wide):
+            at = pl.multiple_of(base + j * wide, wide)
+            part[pl.ds(at, wide), :] = lax.dot_general(
+                tok2[:, pl.ds(at, wide)], cot2[...], (((0,), (0,)), ((), ())), preferred_element_type=F32
+            )
+        for i in range(group):
+            ordered(first_sends, k + i)
+
+    gather_hop(1)
+    for k in range(nz):
+        ordered(second_sends, k)
+    for k in range(2, nz):
+        gather_hop(k)
 
     def own_at(xx, start):
         return pl.ds(pl.multiple_of((z * 4 + xx * 2 + c) * R + start, 16), low if start == 0 else high)
 
-    for d in (0, 1):
-        @pl.when((z > 0) if d == 0 else (z < nz - 1))
-        def _():
-            red_zb(d, z).wait_recv()
-            for xx in (0, 1):
-                part[own_at(xx, low), :] += zr_b[d, z, xx].astype(F32)
-
+    def sum_b(k, carry):
+        source = lax.rem(z + k, nz)
+        red_zb(z, source).wait_recv()
+        for xx in (0, 1):
+            part[own_at(xx, low), :] += zr_b[source, xx].astype(F32)
+        return carry
+
+    lax.fori_loop(1, nz, sum_b, 0)
     red_bx = remote(xs_b, xr_b, rbx_s, rbx_r, x_dev)
     xs_b[...] = mine(z, 1 - x, low, high).astype(BF)
     red_bx.start()
     red_x(z).wait_recv()
     part[own_at(x, 0), :] += xr_a[z].astype(F32)
-    for d in (0, 1):
-        @pl.when((z > 0) if d == 0 else (z < nz - 1))
-        def _():
-            red_za(d, z).wait_recv()
-            part[own_at(x, 0), :] += zr_a[d, z].astype(F32)
-
+
+    def sum_a(k, carry):
+        source = lax.rem(z + k, nz)
+        red_za(z, source).wait_recv()
+        part[own_at(x, 0), :] += zr_a[source].astype(F32)
+        return carry
+
+    lax.fori_loop(1, nz, sum_a, 0)
     loads[3].wait()
     loads[4].wait()
 
@@ -323,27 +278,30 @@
         ys.extend(pair)
 
     optimize(0, 0, low)
+    slots = [lax.rem(z // group + g, nz // group) for g in range(nz // group)]
+
+    def pass_on(slot):
+        for i in range(group):
+            zz = slot * group + i
+            a_x_in(zz).wait_recv()
+            core_a(zz, c).start()
+
+    pass_on(slots[0])
     red_bx.wait_recv()
     part[own_at(x, low), :] += xr_b[...].astype(F32)
     optimize(1, low, high)
 
-    for zz in range(nz):
-        a_x_in(zz).wait_recv()
-        core_a(zz, c).start()
-    group = 1
-    while (group * 4 * R) % 128:
-        group += 1
-    rows = group * 4 * R
-    tokens = tok2[0:T, :]
     upstream = cot2[0:T, :]
     total = jnp.zeros((T, H), F32)
-    for first in range(0, nz, group):
-        for zz in range(first, first + group):
-            core_a(zz, 1 - c).wait_recv()
-            core_b(zz, 1 - c).wait_recv()
-        block = wfull[first : first + group].reshape(rows, H)
-        span = slice(first * 4 * R, first * 4 * R + rows)
-        total += jnp.dot(tokens[:, span], block, preferred_element_type=F32)
+    for g, slot in enumerate(slots):
+        if g > 0:
+            pass_on(slot)
+        for i in range(group):
+            core_a(slot * group + i, 1 - c).wait_recv()
+            core_b(slot * group + i, 1 - c).wait_recv()
+        block = wfull[pl.ds(slot * group, group)].reshape(rows, H)
+        span = pl.ds(pl.multiple_of(slot * rows, rows), rows)
+        total += jnp.dot(tok2[0:T, span], block, preferred_element_type=F32)
         ig_o[:, span] = (
             lax.dot_general(upstream, block, (((1,), (1,)), ((), ())), preferred_element_type=F32) * factor
         ).astype(BF)
@@ -379,10 +337,10 @@
                 a_z(d, zz).wait_send()
                 b_z(d, zz).wait_send()
 
-            @pl.when((zz > z) if d == 0 else (zz < z))
-            def _():
-                red_za(d, zz).wait_send()
-                red_zb(d, zz).wait_send()
+        @pl.when(zz != z)
+        def _():
+            red_za(zz, z).wait_send()
+            red_zb(zz, z).wait_send()
 
 
 def put_out(*refs):
@@ -399,13 +357,14 @@
     _, R, H = weights.shape
     n = nz * 4
     factor = 1.0 / math.sqrt(D)
-    cut = 16 * max(1, round(R / 16 * 5 / 9))
+    keep = 16 * max(1, min(R // 16 - 1, round(R / 16 * 7 / 9)))
+    cut = 16 * max(1, min(R // 16 - 1, round(R / 16 * 8 / 9)))
     high = R - cut
     dma = pltpu.SemaphoreType.DMA
     vmem = pl.BlockSpec(memory_space=pltpu.VMEM)
     hbm = pl.BlockSpec(memory_space=pl.ANY)
     outs = pl.pallas_call(
-        functools.partial(kernel, nz, nb, cut, factor),
+        functools.partial(kernel, nz, nb, keep, cut, factor),
         out_shape=(
             jax.ShapeDtypeStruct((T, H), BF),
             jax.ShapeDtypeStruct((T, D), BF),
@@ -426,10 +385,10 @@
             pltpu.VMEM((D, H), F32),
             pltpu.VMEM((nz, cut, H), BF),
             pltpu.VMEM((nz, cut, H), BF),
-            pltpu.VMEM((2, nz, cut, H), BF),
-            pltpu.VMEM((2, nz, cut, H), BF),
-            pltpu.VMEM((2, nz, 2, high, H), BF),
-            pltpu.VMEM((2, nz, 2, high, H), BF),
+            pltpu.VMEM((nz, cut, H), BF),
+            pltpu.VMEM((nz, cut, H), BF),
+            pltpu.VMEM((nz, 2, high, H), BF),
+            pltpu.VMEM((nz, 2, high, H), BF),
             pltpu.VMEM((high, H), BF),
             pltpu.VMEM((high, H), BF),
             pltpu.VMEM((R, H), BF),
@@ -443,22 +402,23 @@
             dma((nz,)), dma((nz,)),
             dma((nz,)), dma((nz,)),
             dma((nz,)), dma((nz,)),
-            dma((2, nz)), dma((2, nz)),
-            dma((2, nz)), dma((2, nz)),
+            dma((nz,)), dma((nz,)),
+            dma((nz,)), dma((nz,)),
             dma, dma,
             dma((2, 2)), dma((2, 2)),
         ],
         compiler_params=pltpu.CompilerParams(
-            collective_id=0, has_side_effects=True
+            collective_id=0, has_side_effects=True, vmem_limit_bytes=48 * 1024 * 1024
         ),
         name="step",
-    )(tokens[0], cotangent[0], weights[0], moment_one[0], moment_two[0], gossip)
+    )(*(pltpu.with_memory_space_constraint(v, pltpu.HBM) for v in (tokens[0], cotangent[0], weights[0], moment_one[0], moment_two[0], gossip)))
     outs = pl.pallas_call(
         put_out,
         out_shape=tuple(jax.ShapeDtypeStruct(out.shape, out.dtype) for out in outs),
         in_specs=[vmem] * 5,
         out_specs=(hbm,) * 5,
         scratch_shapes=[dma((5,))],
+        compiler_params=pltpu.CompilerParams(vmem_limit_bytes=16 * 1024 * 1024),
         name="put_out",
     )(*outs)
     return tuple(out[None] for out in outs)

time: 41.5 us -> 38.7 us (0.933)
  Pallas kernels: 40.7 us -> 37.9 us
    pallas_call x1, Pallas kernels: 38.2 us -> 36.7 us  [local(): pl.pallas_call(functools.partial(kernel, nz, nb, keep, cut, factor), out_...]
    pallas_call x1, Pallas kernels: 2.55 us -> 1.19 us  [local(): pl.pallas_call(put_out, out_shape=tuple((jax.ShapeDtypeStruct(out.shape,...]
where the time goes in v3:
time: 38.7 us; the launch traced here: 38.5 us
  Pallas kernels  37.9 us (98%)
  between operations  0.64 us (2%)
    pallas_call x1, Pallas kernels, local(): pl.pallas_call(functools.partial(kernel, nz, nb, keep, cut, factor), out_...  36.7 us
    pallas_call x1, Pallas kernels, local(): pl.pallas_call(put_out, out_shape=tuple((jax.ShapeDtypeStruct(out.shape,...  1.19 us

profile of v3, /device:TPU:0, one launch (start us, length us, event | category | flops | bytes accessed | tf_op | source)
XLA Modules:
  0.0 38.5 jit_solution(9362638101739735386)
XLA Ops:
  0.6 36.7 %step.1 = (bf16[128,512]{1,0:T(8,128)(2,1)S(1)}, bf16[128,2304]{1,0:T(8,128)(2,1)S(1)}, f32[144,512]{1,0:T(8,128)S(1)}, f32[144,512]{1,0:T(8,128)S(1)}, f32[144,512]{1,0:T(8,128)S(1)}) custom-call(bf16[128,2304]{1,0:T(8,128)(2,1)} %bitcast.10, bf16[128,512]{1,0:T(8,128)(2,1)} %bitcast.14, f32[144,512]{1,0:T(8,128)} %bitcast.11, f32[144,512]{1,0:T(8,128)} %bitcast.12, ...), custom_call_target="tpu_custom_call" | custom-call | tf_op jit(solution)/shard_map/step/pallas_call | solution.py:366
  37.3 1.2 %put_out.1 = (bf16[128,512]{1,0:T(8,128)(2,1)}, bf16[128,2304]{1,0:T(8,128)(2,1)}, f32[144,512]{1,0:T(8,128)}, f32[144,512]{1,0:T(8,128)}, f32[144,512]{1,0:T(8,128)}) custom-call(bf16[128,512]{1,0:T(8,128)(2,1)S(1)} %get-tuple-element.15.refs_0_, bf16[128,2304]{1,0:T(8,128)(2,1)S(1)} %get-tuple-element.16.refs_1_, ...), custom_call_target="tpu_custom_call" | custom-call | tf_op jit(solution)/shard_map/put_out/pallas_call | solution.py:415

commit v4 on v2

--- a/solution.py
+++ b/solution.py
@@ -399,7 +399,7 @@
     _, R, H = weights.shape
     n = nz * 4
     factor = 1.0 / math.sqrt(D)
-    cut = 16 * max(1, round(R / 16 * 5 / 9))
+    cut = 16 * max(1, round(R / 16 * 7 / 9))
     high = R - cut
     dma = pltpu.SemaphoreType.DMA
     vmem = pl.BlockSpec(memory_space=pltpu.VMEM)
@@ -449,16 +449,17 @@
             dma((2, 2)), dma((2, 2)),
         ],
         compiler_params=pltpu.CompilerParams(
-            collective_id=0, has_side_effects=True
+            collective_id=0, has_side_effects=True, vmem_limit_bytes=48 * 1024 * 1024
         ),
         name="step",
-    )(tokens[0], cotangent[0], weights[0], moment_one[0], moment_two[0], gossip)
+    )(*(pltpu.with_memory_space_constraint(v, pltpu.HBM) for v in (tokens[0], cotangent[0], weights[0], moment_one[0], moment_two[0], gossip)))
     outs = pl.pallas_call(
         put_out,
         out_shape=tuple(jax.ShapeDtypeStruct(out.shape, out.dtype) for out in outs),
         in_specs=[vmem] * 5,
         out_specs=(hbm,) * 5,
         scratch_shapes=[dma((5,))],
+        compiler_params=pltpu.CompilerParams(vmem_limit_bytes=16 * 1024 * 1024),
         name="put_out",
     )(*outs)
     return tuple(out[None] for out in outs)

time: 41.5 us -> 35.3 us (0.85)
  Pallas kernels: 40.7 us -> 34.5 us
    pallas_call x1, Pallas kernels: 38.2 us -> 33.3 us  [local(): pl.pallas_call(functools.partial(kernel, nz, nb, cut, factor), out_shape=...]
    pallas_call x1, Pallas kernels: 2.55 us -> 1.19 us  [local(): pl.pallas_call(put_out, out_shape=tuple((jax.ShapeDtypeStruct(out.shape,...]
where the time goes in v4:
time: 35.3 us; the launch traced here: 35.1 us
  Pallas kernels  34.5 us (98%)
  between operations  0.64 us (2%)
    pallas_call x1, Pallas kernels, local(): pl.pallas_call(functools.partial(kernel, nz, nb, cut, factor), out_shape=...  33.3 us
    pallas_call x1, Pallas kernels, local(): pl.pallas_call(put_out, out_shape=tuple((jax.ShapeDtypeStruct(out.shape,...  1.19 us

profile of v4, /device:TPU:0, one launch (start us, length us, event | category | flops | bytes accessed | tf_op | source)
XLA Modules:
  0.0 35.1 jit_solution(8673911360529941177)
XLA Ops:
  0.6 33.3 %step.1 = (bf16[128,512]{1,0:T(8,128)(2,1)S(1)}, bf16[128,2304]{1,0:T(8,128)(2,1)S(1)}, f32[144,512]{1,0:T(8,128)S(1)}, f32[144,512]{1,0:T(8,128)S(1)}, f32[144,512]{1,0:T(8,128)S(1)}) custom-call(bf16[128,2304]{1,0:T(8,128)(2,1)} %bitcast.10, bf16[128,512]{1,0:T(8,128)(2,1)} %bitcast.14, f32[144,512]{1,0:T(8,128)} %bitcast.11, f32[144,512]{1,0:T(8,128)} %bitcast.12, ...), custom_call_target="tpu_custom_call" | custom-call | tf_op jit(solution)/shard_map/step/pallas_call | solution.py:407
  33.9 1.2 %put_out.1 = (bf16[128,512]{1,0:T(8,128)(2,1)}, bf16[128,2304]{1,0:T(8,128)(2,1)}, f32[144,512]{1,0:T(8,128)}, f32[144,512]{1,0:T(8,128)}, f32[144,512]{1,0:T(8,128)}) custom-call(bf16[128,512]{1,0:T(8,128)(2,1)S(1)} %get-tuple-element.15.refs_0_, bf16[128,2304]{1,0:T(8,128)(2,1)S(1)} %get-tuple-element.16.refs_1_, ...), custom_call_target="tpu_custom_call" | custom-call | tf_op jit(solution)/shard_map/put_out/pallas_call | solution.py:456
